TPU v7x, 256 devices: a whole 4x4x8 slice. The times are simulated.
256 devices in a mesh: sec: 16 (over z, core), term: 16 (over y, x).
Axes of the slice: x: 4, y: 4, z: 8, core: 2. Of those that a mesh axis runs over, the one named last changes fastest.
Arguments:
- psi: bfloat16 [16, 512, 512], P('sec'), may hold values from -6 to 6
- left_ops: bfloat16 [16, 96, 512, 512], P('sec', 'term'), may hold values from -0.078125 to 0.078125
- right_ops: bfloat16 [16, 96, 512, 512], P('sec', 'term'), may hold values from -0.078125 to 0.078125
- term_mask: int32 [16, 96], P('sec', 'term'), may hold values 0 or 1
- pair_src: int32 [16], P('sec'), may hold values from 0 to 15, each once
- pair_dst: int32 [16], P('sec'), may hold values from 0 to 15, each once
Outputs:
- sigma: bfloat16 [16, 512, 512], P('sec')
Inputs may be any that keep to these rules, and one draw needn't show every extreme that they name: `pair_src`: each of the 16 sector blocks is the source of exactly one pair. `pair_dst`: each of the 16 sector blocks is the target of exactly one pair.
All inputs are finite; a program needn't handle non-finite values. No bound on the sum of `term_mask` on one device may be relied on, other than what follows from the above.
Results may differ from a plain program's by a relative error of at most 0.0065.
Values may be sent and summed in bfloat16 or wider, within the bound.
A program may use at most 64 MiB of HBM per device.

v0:
```python
import jax
import jax.numpy as jnp
from jax import lax
from jax.sharding import PartitionSpec as P


def in_blocks(value, dim, peers):
    shape = value.shape
    pieces = value.reshape(*shape[:dim], peers, shape[dim] // peers, *shape[dim + 1 :])
    return jnp.moveaxis(pieces, dim, 0)


def sent_and_summed(value, axis, dim):
    pieces = in_blocks(value, dim, lax.axis_size(axis))
    arrived = lax.all_to_all(pieces, axis, split_axis=0, concat_axis=0, tiled=True)
    return arrived.astype(jnp.float32).sum(axis=0)


def in_one_piece(arrays, axis, dim, along):
    columns = [a.reshape(*a.shape[:along], -1) for a in arrays]
    both = jnp.concatenate(columns, axis=along)
    filled, at, finished = (lax.all_gather(both, axis, axis=dim, tiled=True), 0, [])
    for a, column in zip(arrays, columns):
        piece = filled[..., at : at + column.shape[along]]
        finished.append(piece.reshape(*piece.shape[:along], *a.shape[along:]))
        at += column.shape[along]
    return tuple(finished)


def in_order(pieces, dim):
    pieces = jnp.moveaxis(pieces, 0, dim)
    shape = pieces.shape
    return pieces.reshape(*shape[:dim], shape[dim] * shape[dim + 1], *shape[dim + 2 :])


def copy_for_each(value, axis):
    peers = lax.axis_size(axis)
    return lax.all_to_all(
        jnp.broadcast_to(value[None], (peers, *value.shape)), axis, 0, 0, tiled=True
    )


def gathered_copies(value, axis, dim):
    return in_order(copy_for_each(value, axis), dim)


def local(psi, left_ops, right_ops, term_mask, pair_src, pair_dst):
    whole = lax.all_gather(psi, "sec", axis=0, tiled=True)
    order = psi.shape[1]
    local_pairs = psi.shape[0]
    local_terms = left_ops.shape[1]
    zero_block = jnp.zeros((order, order), jnp.float32)
    source = pair_src[0]
    target = pair_dst[0]
    src_block = lax.dynamic_index_in_dim(whole, source, 0, keepdims=False)
    dst_block = lax.dynamic_index_in_dim(whole, target, 0, keepdims=False)

    def term_step(acc, term):

        def active(carry):
            fwd_acc, adj_acc = carry
            left = left_ops[0, term]
            right = right_ops[0, term]
            inner_fwd = jnp.dot(left, src_block, preferred_element_type=jnp.float32).astype(
                jnp.bfloat16
            )
            inner_adj = jnp.dot(left.T, dst_block, preferred_element_type=jnp.float32).astype(
                jnp.bfloat16
            )
            fwd_acc = fwd_acc + jnp.dot(inner_fwd, right.T, preferred_element_type=jnp.float32)
            adj_acc = adj_acc + jnp.dot(inner_adj, right, preferred_element_type=jnp.float32)
            return (fwd_acc, adj_acc)

        return (lax.cond(term_mask[0, term] == 1, active, lambda carry: carry, acc), None)

    (fwd, adj), _ = lax.scan(
        term_step, (zero_block, zero_block), jnp.arange(local_terms, dtype=jnp.int32)
    )
    fwd_list = [fwd]
    adj_list = [adj]
    stacked = jnp.stack([jnp.stack(fwd_list), jnp.stack(adj_list)], axis=1)
    pieces = sent_and_summed(stacked.astype(jnp.bfloat16), "term", 2)
    all_pieces, all_src, all_dst = in_one_piece(
        (pieces, pair_src.astype(jnp.float32), pair_dst.astype(jnp.float32)), "sec", 0, 1
    )
    mine = (lax.axis_index("sec") * local_pairs + jnp.arange(local_pairs, dtype=jnp.int32)).astype(
        jnp.float32
    )
    pick_fwd = (all_dst[None, :] == mine[:, None]).astype(jnp.float32)
    pick_adj = (all_src[None, :] == mine[:, None]).astype(jnp.float32)
    rows_fwd = jnp.einsum(
        "sk,krc->src", pick_fwd, all_pieces[:, 0], precision=lax.Precision.HIGHEST
    )
    rows_adj = jnp.einsum(
        "sk,krc->src", pick_adj, all_pieces[:, 1], precision=lax.Precision.HIGHEST
    )
    rows = (rows_fwd + rows_adj).astype(jnp.bfloat16)
    return gathered_copies(rows, "term", 1)


def solution(mesh):
    placed = (
        P("sec", None, None),
        P("sec", "term", None, None),
        P("sec", "term", None, None),
        P("sec", "term"),
        P("sec"),
        P("sec"),
    )
    return jax.shard_map(
        local, mesh=mesh, in_specs=placed, out_specs=P("sec", None, None), check_vma=False
    )
```

profile of v0, /device:TPU:1, one launch (start us, length us, event | category | flops | bytes accessed | tf_op | source)
XLA Modules:
  0.0 217.1 jit_solution(3146875595708951832)
XLA Ops:
  8.6 60.7 %all-gather.4.cloned.1.call-done = bf16[16,512,512]{2,1,0:T(8,128)(2,1)} async-done(((bf16[1,512,512]{2,1,0:T(8,128)(2,1)}), bf16[16,512,512]{2,1,0:T(8,128)(2,1)}) %all-gather.4.cloned.1.call-update) | async-done | bytes 8388624 | tf_op jit(solution)/shard_map/all_gather | solution.py:48
  69.2 1.3 dynamic-slice_bitcast_fusion
  70.8 53.7 %while.12 = (s32[]{:T(128)}, f32[512,512]{1,0:T(8,128)S(1)}, f32[512,512]{1,0:T(8,128)S(1)}, s32[6]{0:T(128)S(1)}, s32[1,6]{1,0:T(1,128)S(1)}, /*index=5*/bf16[1...) while((s32[]{:T(128)}, f32[512,512]{1,0:T(8,128)S(1)}, ...), condition=%wide.region_3.4_spmd, body=%wide.region_0.3_spmd.sunk | while | flops 1074790400 | bytes 7342387 | solution.py:76
  74.7 6.0 %conditional.2 = ((f32[512,512]{1,0:T(8,128)S(1)}, f32[512,512]{1,0:T(8,128)S(1)})) conditional(s32[]{:T(128)} %bitcast.55, (f32[512,512]{1,0:T(8,128)S(1)}, f32[512,512]{1,0:T(8,128)S(1)}) %tuple.30, (s32[]{:T(128)}, bf16[1,6,512,512]{3,2,1,0:T(8,128)(2,1)}, bf16[512,512]{1,0:T(8,128)(2,1)S(1)}, bf16[1,6,512,512]{3,2,1,0:T(8,128)(2,1)}, ...), branch_computations={%region_1.1_spmd, %region_2.2_spmd} | conditional | flops 1074790400 | bytes 7342138 | solution.py:74
  76.8 1.9 convolution_add_fusion
  78.8 1.9 convolution_add_fusion.1
  84.7 6.0 %conditional.2 = ((f32[512,512]{1,0:T(8,128)S(1)}, f32[512,512]{1,0:T(8,128)S(1)})) conditional(s32[]{:T(128)} %bitcast.55, (f32[512,512]{1,0:T(8,128)S(1)}, f32[512,512]{1,0:T(8,128)S(1)}) %tuple.30, (s32[]{:T(128)}, bf16[1,6,512,512]{3,2,1,0:T(8,128)(2,1)}, bf16[512,512]{1,0:T(8,128)(2,1)S(1)}, bf16[1,6,512,512]{3,2,1,0:T(8,128)(2,1)}, ...), branch_computations={%region_1.1_spmd, %region_2.2_spmd} | conditional | flops 1074790400 | bytes 7342138 | solution.py:74
  86.7 1.9 convolution_add_fusion
  88.7 1.9 convolution_add_fusion.1
  94.6 6.0 %conditional.2 = ((f32[512,512]{1,0:T(8,128)S(1)}, f32[512,512]{1,0:T(8,128)S(1)})) conditional(s32[]{:T(128)} %bitcast.55, (f32[512,512]{1,0:T(8,128)S(1)}, f32[512,512]{1,0:T(8,128)S(1)}) %tuple.30, (s32[]{:T(128)}, bf16[1,6,512,512]{3,2,1,0:T(8,128)(2,1)}, bf16[512,512]{1,0:T(8,128)(2,1)S(1)}, bf16[1,6,512,512]{3,2,1,0:T(8,128)(2,1)}, ...), branch_computations={%region_1.1_spmd, %region_2.2_spmd} | conditional | flops 1074790400 | bytes 7342138 | solution.py:74
  96.7 2.0 convolution_add_fusion
  98.6 1.9 convolution_add_fusion.1
  108.6 6.0 %conditional.2 = ((f32[512,512]{1,0:T(8,128)S(1)}, f32[512,512]{1,0:T(8,128)S(1)})) conditional(s32[]{:T(128)} %bitcast.55, (f32[512,512]{1,0:T(8,128)S(1)}, f32[512,512]{1,0:T(8,128)S(1)}) %tuple.30, (s32[]{:T(128)}, bf16[1,6,512,512]{3,2,1,0:T(8,128)(2,1)}, bf16[512,512]{1,0:T(8,128)(2,1)S(1)}, bf16[1,6,512,512]{3,2,1,0:T(8,128)(2,1)}, ...), branch_computations={%region_1.1_spmd, %region_2.2_spmd} | conditional | flops 1074790400 | bytes 7342138 | solution.py:74
  110.6 1.9 convolution_add_fusion
  112.6 1.9 convolution_add_fusion.1
  118.5 6.0 %conditional.2 = ((f32[512,512]{1,0:T(8,128)S(1)}, f32[512,512]{1,0:T(8,128)S(1)})) conditional(s32[]{:T(128)} %bitcast.55, (f32[512,512]{1,0:T(8,128)S(1)}, f32[512,512]{1,0:T(8,128)S(1)}) %tuple.30, (s32[]{:T(128)}, bf16[1,6,512,512]{3,2,1,0:T(8,128)(2,1)}, bf16[512,512]{1,0:T(8,128)(2,1)S(1)}, bf16[1,6,512,512]{3,2,1,0:T(8,128)(2,1)}, ...), branch_computations={%region_1.1_spmd, %region_2.2_spmd} | conditional | flops 1074790400 | bytes 7342138 | solution.py:74
  120.6 1.9 convolution_add_fusion
  122.5 1.9 convolution_add_fusion.1
  125.7 6.3 %all-to-all-start = ((bf16[16,1,2,32,512]{4,3,2,1,0:T(8,128)(2,1)}), bf16[16,1,2,32,512]{4,3,2,1,0:T(8,128)(2,1)S(1)}, u32[]{:S(2)}, u32[]{:S(2)}) async-start(bf16[16,1,2,32,512]{4,3,2,1,0:T(8,128)(2,1)} %maximum_bitcast_fusion), calls=%async_computation | async-start | bytes 2097152 | tf_op jit(solution)/shard_map/all_to_all | solution.py:15
  132.0 16.1 %all-to-all-done = bf16[16,1,2,32,512]{4,3,2,1,0:T(8,128)(2,1)S(1)} async-done(((bf16[16,1,2,32,512]{4,3,2,1,0:T(8,128)(2,1)}), bf16[16,1,2,32,512]{4,3,2,1,0:T(8,128)(2,1)S(1)}, u32[]{:S(2)}, u32[]{:S(2)}) %all-to-all-start) | async-done | bytes 1048608 | tf_op jit(solution)/shard_map/all_to_all | solution.py:15
  149.3 37.2 %all-gather.6.cloned.1.call-done = f32[16,1,32770]{2,1,0:T(1,128)} async-done(((f32[1,1,32770]{2,1,0:T(1,128)}), f32[16,1,32770]{2,1,0:T(1,128)}) %all-gather.6.cloned.1.call-update) | async-done | bytes 2097296 | tf_op jit(solution)/shard_map/all_gather | solution.py:22
  186.5 1.7 copy.20
  188.4 1.2 copy.12
  192.3 17.1 %all_to_all.10 = bf16[16,1,32,512]{3,2,1,0:T(8,128)(2,1)S(1)} all-to-all(bf16[16,1,32,512]{3,2,1,0:T(8,128)(2,1)S(1)} %broadcast_in_dim.5), channel_id=1, replica_groups=mesh['sec'=16,'term'=16] {'term'}, dimensions={0} | all-to-all | bytes 1048576 | tf_op jit(solution)/shard_map/all_to_all | solution.py:38
  (40 shorter events, 14.6 us)
Async XLA Ops:
  6.5 64.2 %copy-start.1 = (s32[1,6]{1,0:T(1,128)S(1)}, s32[1,6]{1,0:T(1,128)}, u32[]{:S(2)}) copy-start(s32[1,6]{1,0:T(1,128)} %param.13) | copy-start | bytes 76
  6.5 62.7 %all-gather.4.cloned.1.call-start = ((), (), s32[]{:S(2)}) async-start(), calls=%async_computation.2 | async-start | bytes 8912896 | tf_op jit(solution)/shard_map/all_gather | solution.py:48
  125.7 22.4 %all-to-all-start = ((bf16[16,1,2,32,512]{4,3,2,1,0:T(8,128)(2,1)}), bf16[16,1,2,32,512]{4,3,2,1,0:T(8,128)(2,1)S(1)}, u32[]{:S(2)}, u32[]{:S(2)}) async-start(bf16[16,1,2,32,512]{4,3,2,1,0:T(8,128)(2,1)} %maximum_bitcast_fusion), calls=%async_computation | async-start | bytes 2097152 | tf_op jit(solution)/shard_map/all_to_all | solution.py:15
  132.0 54.5 %all-gather.6.cloned.1.call-start = ((), (), s32[]{:S(2)}) async-start(), calls=%async_computation.3 | async-start | bytes 2236928 | tf_op jit(solution)/shard_map/all_gather | solution.py:22
  148.6 0.7 copy-start
Sparse Core Ops, SparseCore 0:
  9.2 60.0 all-gather.3
  149.4 37.0 all-gather.5
where the time goes:
time: 218 us; the launch traced here: 217 us
  waiting for transfers between devices  115 us (53%)
  loops' own time  26.7 us (12%)
  matrix products  21.6 us (10%)
  blocking collectives  17.1 us (8%)
  between operations  14.9 us (7%)
  local copies, waits for them, and re-layouts  10.6 us (5%)
  starting transfers between devices  6.3 us (3%)
  other arithmetic  5.21 us (2%)
    all_gather x1, waiting for transfers between devices, local(): whole = lax.all_gather(psi, 'sec', axis=0, tiled=True)  60.7 us
    all_gather x1, waiting for transfers between devices, in_one_piece(): lax.all_gather(both, axis, axis=dim, tiled=True)  37.2 us
    all_to_all x1, blocking collectives, copy_for_each(): lax.all_to_all(jnp.broadcast_to(value[None], (peers, *value.shape)), axis...  17.1 us
    another operation x1, loops' own time, local(): lax.scan(term_step, (zero_block, zero_block), jnp.arange(local_terms, dty...  16.3 us
    all_to_all x1, waiting for transfers between devices, sent_and_summed(): lax.all_to_all(pieces, axis, split_axis=0, concat_axis=0, tiled=True)  16.1 us
    another operation x6, loops' own time, term_step(): lax.cond(term_mask[0, term] == 1, active, lambda carry: carry, acc)  10.4 us
    dot_general x5, matrix products, active(): jnp.dot(inner_adj, right, preferred_element_type=jnp.float32)  9.73 us
    dot_general x5, matrix products, active(): jnp.dot(inner_fwd, right.T, preferred_element_type=jnp.float32)  9.7 us
  transfers between devices with their start and end apart: 3, of which 3 were waited for; matrix products, arithmetic and copies ran while one was open for 0% of the time, Pallas kernels for 0%

commit v1 on v0

--- a/solution.py
+++ b/solution.py
@@ -45,7 +45,9 @@
 
 
 def local(psi, left_ops, right_ops, term_mask, pair_src, pair_dst):
-    whole = lax.all_gather(psi, "sec", axis=0, tiled=True)
+    whole = jnp.concatenate(
+        lax.all_to_all(jnp.stack([psi] * lax.axis_size("sec")), "sec", 0, 0), axis=0
+    )
     order = psi.shape[1]
     local_pairs = psi.shape[0]
     local_terms = left_ops.shape[1]

time: 218 us -> 351 us (1.61)
  waiting for transfers between devices: 115 us -> 236 us
  starting transfers between devices: 6.3 us -> 16.6 us
  local copies, waits for them, and re-layouts: 10.6 us -> 15.2 us
  loops' own time: 26.7 us -> 22.6 us
    all_to_all x0 -> x1, waiting for transfers between devices: none -> 182 us  [local(): lax.all_to_all(jnp.stack([psi] * lax.axis_size('sec')), 'sec', 0, 0)]
    all_gather x1 -> x0, waiting for transfers between devices: 60.7 us -> none  [local(): whole = lax.all_gather(psi, 'sec', axis=0, tiled=True)]
    all_to_all x0 -> x1, starting transfers between devices: none -> 9.97 us  [local(): lax.all_to_all(jnp.stack([psi] * lax.axis_size('sec')), 'sec', 0, 0)]
    another operation x0 -> x1, local copies, waits for them, and re-layouts: none -> 5.07 us  [local(): jnp.stack([psi] * lax.axis_size('sec'))]
where the time goes in v1:
time: 351 us; the launch traced here: 350 us
  waiting for transfers between devices  236 us (67%)
  loops' own time  22.6 us (6%)
  matrix products  21.6 us (6%)
  blocking collectives  17.1 us (5%)
  starting transfers between devices  16.6 us (5%)
  local copies, waits for them, and re-layouts  15.2 us (4%)
  between operations  14.9 us (4%)
  other arithmetic  5.37 us (2%)
    all_to_all x1, waiting for transfers between devices, local(): lax.all_to_all(jnp.stack([psi] * lax.axis_size('sec')), 'sec', 0, 0)  182 us
    all_gather x1, waiting for transfers between devices, in_one_piece(): lax.all_gather(both, axis, axis=dim, tiled=True)  38.9 us
    all_to_all x1, blocking collectives, copy_for_each(): lax.all_to_all(jnp.broadcast_to(value[None], (peers, *value.shape)), axis...  17.1 us
    all_to_all x1, waiting for transfers between devices, sent_and_summed(): lax.all_to_all(pieces, axis, split_axis=0, concat_axis=0, tiled=True)  15.5 us
    another operation x1, loops' own time, local(): lax.scan(term_step, (zero_block, zero_block), jnp.arange(local_terms, dty...  14 us
    all_to_all x1, starting transfers between devices, local(): lax.all_to_all(jnp.stack([psi] * lax.axis_size('sec')), 'sec', 0, 0)  9.97 us
    dot_general x5, matrix products, active(): jnp.dot(inner_adj, right, preferred_element_type=jnp.float32)  9.73 us
    dot_general x5, matrix products, active(): jnp.dot(inner_fwd, right.T, preferred_element_type=jnp.float32)  9.7 us
  transfers between devices with their start and end apart: 3, of which 3 were waited for; matrix products, arithmetic and copies ran while one was open for 0% of the time, Pallas kernels for 0%

profile of v1, /device:TPU:1, one launch (start us, length us, event | category | flops | bytes accessed | tf_op | source)
XLA Modules:
  0.0 349.9 jit_solution(2312460628661837069)
XLA Ops:
  6.5 5.1 %stack.8 = bf16[16,1,512,512]{3,2,1,0:T(8,128)(2,1)} broadcast(bf16[512,512]{1,0:T(8,128)(2,1)} %bitcast.71), dimensions={2,3} | broadcast | bytes 8912896 | tf_op jit(solution)/shard_map/stack | solution.py:49
  11.6 10.0 %all-to-all-start = ((bf16[16,1,512,512]{3,2,1,0:T(8,128)(2,1)}), bf16[16,1,512,512]{3,2,1,0:T(8,128)(2,1)}, u32[]{:S(2)}, u32[]{:S(2)}) async-start(bf16[16,1,512,512]{3,2,1,0:T(8,128)(2,1)} %stack.8), calls=%async_computation | async-start | bytes 16777216 | tf_op jit(solution)/shard_map/all_to_all | solution.py:49
  22.9 182.1 %all-to-all-done = bf16[16,1,512,512]{3,2,1,0:T(8,128)(2,1)} async-done(((bf16[16,1,512,512]{3,2,1,0:T(8,128)(2,1)}), bf16[16,1,512,512]{3,2,1,0:T(8,128)(2,1)}, u32[]{:S(2)}, u32[]{:S(2)}) %all-to-all-start) | async-done | bytes 8388640 | tf_op jit(solution)/shard_map/all_to_all | solution.py:49
  206.5 49.3 %while.12 = (s32[]{:T(128)}, f32[512,512]{1,0:T(8,128)S(1)}, f32[512,512]{1,0:T(8,128)S(1)}, s32[6]{0:T(128)S(1)}, s32[1,6]{1,0:T(1,128)S(1)}, /*index=5*/bf16[1...) while((s32[]{:T(128)}, f32[512,512]{1,0:T(8,128)S(1)}, ...), condition=%wide.region_3.4_spmd, body=%wide.region_0.3_spmd.sunk | while | flops 1074790400 | bytes 7342387 | solution.py:78
  210.1 5.6 %conditional.2 = ((f32[512,512]{1,0:T(8,128)S(1)}, f32[512,512]{1,0:T(8,128)S(1)})) conditional(s32[]{:T(128)} %bitcast.56, (f32[512,512]{1,0:T(8,128)S(1)}, f32[512,512]{1,0:T(8,128)S(1)}) %tuple.30, (s32[]{:T(128)}, bf16[1,6,512,512]{3,2,1,0:T(8,128)(2,1)}, bf16[512,512]{1,0:T(8,128)(2,1)S(1)}, bf16[1,6,512,512]{3,2,1,0:T(8,128)(2,1)}, ...), branch_computations={%region_1.1_spmd, %region_2.2_spmd} | conditional | flops 1074790400 | bytes 7342138 | solution.py:76
  211.8 1.9 convolution_add_fusion
  213.7 1.9 convolution_add_fusion.1
  219.2 5.6 %conditional.2 = ((f32[512,512]{1,0:T(8,128)S(1)}, f32[512,512]{1,0:T(8,128)S(1)})) conditional(s32[]{:T(128)} %bitcast.56, (f32[512,512]{1,0:T(8,128)S(1)}, f32[512,512]{1,0:T(8,128)S(1)}) %tuple.30, (s32[]{:T(128)}, bf16[1,6,512,512]{3,2,1,0:T(8,128)(2,1)}, bf16[512,512]{1,0:T(8,128)(2,1)S(1)}, bf16[1,6,512,512]{3,2,1,0:T(8,128)(2,1)}, ...), branch_computations={%region_1.1_spmd, %region_2.2_spmd} | conditional | flops 1074790400 | bytes 7342138 | solution.py:76
  220.9 1.9 convolution_add_fusion
  222.9 1.9 convolution_add_fusion.1
  228.4 5.6 %conditional.2 = ((f32[512,512]{1,0:T(8,128)S(1)}, f32[512,512]{1,0:T(8,128)S(1)})) conditional(s32[]{:T(128)} %bitcast.56, (f32[512,512]{1,0:T(8,128)S(1)}, f32[512,512]{1,0:T(8,128)S(1)}) %tuple.30, (s32[]{:T(128)}, bf16[1,6,512,512]{3,2,1,0:T(8,128)(2,1)}, bf16[512,512]{1,0:T(8,128)(2,1)S(1)}, bf16[1,6,512,512]{3,2,1,0:T(8,128)(2,1)}, ...), branch_computations={%region_1.1_spmd, %region_2.2_spmd} | conditional | flops 1074790400 | bytes 7342138 | solution.py:76
  230.1 1.9 convolution_add_fusion
  232.0 1.9 convolution_add_fusion.1
  241.1 5.6 %conditional.2 = ((f32[512,512]{1,0:T(8,128)S(1)}, f32[512,512]{1,0:T(8,128)S(1)})) conditional(s32[]{:T(128)} %bitcast.56, (f32[512,512]{1,0:T(8,128)S(1)}, f32[512,512]{1,0:T(8,128)S(1)}) %tuple.30, (s32[]{:T(128)}, bf16[1,6,512,512]{3,2,1,0:T(8,128)(2,1)}, bf16[512,512]{1,0:T(8,128)(2,1)S(1)}, bf16[1,6,512,512]{3,2,1,0:T(8,128)(2,1)}, ...), branch_computations={%region_1.1_spmd, %region_2.2_spmd} | conditional | flops 1074790400 | bytes 7342138 | solution.py:76
  242.8 1.9 convolution_add_fusion
  244.7 1.9 convolution_add_fusion.1
  250.2 5.6 %conditional.2 = ((f32[512,512]{1,0:T(8,128)S(1)}, f32[512,512]{1,0:T(8,128)S(1)})) conditional(s32[]{:T(128)} %bitcast.56, (f32[512,512]{1,0:T(8,128)S(1)}, f32[512,512]{1,0:T(8,128)S(1)}) %tuple.30, (s32[]{:T(128)}, bf16[1,6,512,512]{3,2,1,0:T(8,128)(2,1)}, bf16[512,512]{1,0:T(8,128)(2,1)S(1)}, bf16[1,6,512,512]{3,2,1,0:T(8,128)(2,1)}, ...), branch_computations={%region_1.1_spmd, %region_2.2_spmd} | conditional | flops 1074790400 | bytes 7342138 | solution.py:76
  251.9 1.9 convolution_add_fusion
  253.9 1.9 convolution_add_fusion.1
  257.0 6.6 %all-to-all-start.1 = ((bf16[16,1,2,32,512]{4,3,2,1,0:T(8,128)(2,1)}), bf16[16,1,2,32,512]{4,3,2,1,0:T(8,128)(2,1)S(1)}, u32[]{:S(2)}, u32[]{:S(2)}) async-start(bf16[16,1,2,32,512]{4,3,2,1,0:T(8,128)(2,1)} %maximum_bitcast_fusion), calls=%async_computation.1 | async-start | bytes 2097152 | tf_op jit(solution)/shard_map/all_to_all | solution.py:15
  263.7 15.5 %all-to-all-done.1 = bf16[16,1,2,32,512]{4,3,2,1,0:T(8,128)(2,1)S(1)} async-done(((bf16[16,1,2,32,512]{4,3,2,1,0:T(8,128)(2,1)}), bf16[16,1,2,32,512]{4,3,2,1,0:T(8,128)(2,1)S(1)}, u32[]{:S(2)}, u32[]{:S(2)}) %all-to-all-start.1) | async-done | bytes 1048608 | tf_op jit(solution)/shard_map/all_to_all | solution.py:15
  280.4 38.9 %all-gather.3.cloned.1.call-done = f32[16,1,32770]{2,1,0:T(1,128)} async-done(((f32[1,1,32770]{2,1,0:T(1,128)}), f32[16,1,32770]{2,1,0:T(1,128)}) %all-gather.3.cloned.1.call-update) | async-done | bytes 2097296 | tf_op jit(solution)/shard_map/all_gather | solution.py:22
  319.3 1.7 copy.20
  325.1 17.1 %all_to_all.15 = bf16[16,1,32,512]{3,2,1,0:T(8,128)(2,1)S(1)} all-to-all(bf16[16,1,32,512]{3,2,1,0:T(8,128)(2,1)S(1)} %broadcast_in_dim.5), channel_id=1, replica_groups=mesh['sec'=16,'term'=16] {'term'}, dimensions={0} | all-to-all | bytes 1048576 | tf_op jit(solution)/shard_map/all_to_all | solution.py:38
  (40 shorter events, 16.0 us)
Async XLA Ops:
  11.6 193.4 %all-to-all-start = ((bf16[16,1,512,512]{3,2,1,0:T(8,128)(2,1)}), bf16[16,1,512,512]{3,2,1,0:T(8,128)(2,1)}, u32[]{:S(2)}, u32[]{:S(2)}) async-start(bf16[16,1,512,512]{3,2,1,0:T(8,128)(2,1)} %stack.8), calls=%async_computation | async-start | bytes 16777216 | tf_op jit(solution)/shard_map/all_to_all | solution.py:49
  21.6 184.9 %copy-start.1 = (s32[1,6]{1,0:T(1,128)S(1)}, s32[1,6]{1,0:T(1,128)}, u32[]{:S(2)}) copy-start(s32[1,6]{1,0:T(1,128)} %param.13) | copy-start | bytes 76
  257.0 22.1 %all-to-all-start.1 = ((bf16[16,1,2,32,512]{4,3,2,1,0:T(8,128)(2,1)}), bf16[16,1,2,32,512]{4,3,2,1,0:T(8,128)(2,1)S(1)}, u32[]{:S(2)}, u32[]{:S(2)}) async-start(bf16[16,1,2,32,512]{4,3,2,1,0:T(8,128)(2,1)} %maximum_bitcast_fusion), calls=%async_computation.1 | async-start | bytes 2097152 | tf_op jit(solution)/shard_map/all_to_all | solution.py:15
  263.6 55.6 %all-gather.3.cloned.1.call-start = ((), (), s32[]{:S(2)}) async-start(), calls=%async_computation.3 | async-start | bytes 2236928 | tf_op jit(solution)/shard_map/all_gather | solution.py:22
  279.7 0.7 copy-start
Sparse Core Ops, SparseCore 0:
  280.5 38.7 all-gather.2
